TPU v7x, 32 devices: a whole 2x2x4 slice. The times are simulated.
32 devices in a mesh: dp: 4 (over z), ctx: 8 (over y, x, core).
Axes of the slice: x: 2, y: 2, z: 4, core: 2. Of those that a mesh axis runs over, the one named last changes fastest.
Arguments:
- tokens: bfloat16 [4, 1024, 8192], P('dp', 'ctx'), may hold values from -6 to 6
- w_down: bfloat16 [8192, 512], P(('dp', 'ctx')), may hold values from -0.0625 to 0.0625
- w_up: bfloat16 [512, 1024], replicated, may hold values from -0.25 to 0.25
- queries: bfloat16 [4, 1024, 4096], P('dp', 'ctx'), may hold values from -70 to 70, as said below
- block_order: int32 [4, 16], P('dp', 'ctx'), may hold values from 0 to 15, each once within a row
Outputs:
- attended: bfloat16 [4, 1024, 4096], P('dp', 'ctx')
Inputs may be any that keep to these rules, and one draw needn't show every extreme that they name: `queries`: query entries.
All inputs are finite; a program needn't handle non-finite values.
Results may differ from a plain program's by a relative error of at most 0.014.
The roundings to bfloat16 on the way count: a program that leaves them out, or rounds other values in their place, can miss the bound.
Values may be sent and summed in bfloat16 or wider, within the bound.
A program may use at most 64 MiB of HBM per device.

v0:
```python
import math
import jax
import jax.numpy as jnp
from jax import lax
from jax.sharding import PartitionSpec as P

QH = 32
KVH = 4
HD = 128


def per_device(tokens, w_down, w_up, queries, block_order):
    local_rows = tokens.shape[1]
    half_rows = local_rows // 2
    features = tokens[0]
    summed = jnp.dot(
        features,
        lax.all_gather(w_down, ("dp", "ctx"), axis=0, tiled=True),
        preferred_element_type=jnp.float32,
    )
    latent = summed.astype(jnp.bfloat16)
    order_whole = lax.all_gather(block_order, "ctx", axis=1, tiled=True)[0]
    block_count = order_whole.shape[0]
    local_ids = jnp.arange(local_rows, dtype=jnp.int32)
    query_pos = (
        jnp.where(local_ids < half_rows, block_order[0, 0], block_order[0, 1]) * half_rows
        + local_ids % half_rows
    )
    group = QH // KVH
    query_heads = queries[0].reshape(local_rows, KVH, group, HD).transpose(1, 2, 0, 3)
    score_scale = HD ** (-0.5)

    def update(carry, kv_block, key_pos):
        running_max, running_total, running_sum = carry
        width = kv_block.shape[0]
        key_block = kv_block[:, : KVH * HD].reshape(width, KVH, HD)
        value_block = kv_block[:, KVH * HD :].reshape(width, KVH, HD)
        scores = (
            jnp.einsum("kgsd,tkd->kgst", query_heads, key_block, preferred_element_type=jnp.float32)
            * score_scale
        )
        allowed = key_pos[None, :] <= query_pos[:, None]
        scores = jnp.where(allowed, scores, -1e30)
        new_max = jnp.maximum(running_max, jnp.max(scores, axis=-1))
        correction = jnp.exp(running_max - new_max)
        expo = jnp.where(allowed, jnp.exp(scores - new_max[..., None]), 0.0)
        new_total = running_total * correction + jnp.sum(expo, axis=-1)
        contrib = jnp.einsum(
            "kgst,tkd->kgsd",
            expo.astype(jnp.bfloat16),
            value_block,
            preferred_element_type=jnp.float32,
        )
        return (new_max, new_total, running_sum * correction[..., None] + contrib)

    start_state = (
        jnp.full((KVH, group, local_rows), -1e30, jnp.float32),
        jnp.zeros((KVH, group, local_rows), jnp.float32),
        jnp.zeros((KVH, group, local_rows, HD), jnp.float32),
    )
    kv_local = jnp.dot(latent, w_up, preferred_element_type=jnp.float32).astype(jnp.bfloat16)
    piece = lax.all_gather(kv_local, "ctx", axis=0, tiled=True)
    count = piece.shape[0]
    width = math.gcd(count, 256)
    blocks = piece.reshape(count // width, width, piece.shape[1])
    row_ids = jnp.arange(count, dtype=jnp.int32)
    onehot = (row_ids // half_rows)[:, None] == jnp.arange(block_count, dtype=jnp.int32)[None, :]
    block_ids = jnp.sum(jnp.where(onehot, order_whole[None, :], 0), axis=1)
    key_positions = (block_ids * half_rows + row_ids % half_rows).reshape(count // width, width)

    def step_block(state, inputs):
        block, key_pos = inputs
        state = update(state, block, key_pos)
        return (state, None)

    result, unused = lax.scan(step_block, start_state, (blocks, key_positions))
    unused_max, final_total, final_sum = result
    outputs = final_sum / final_total[..., None]
    return outputs.transpose(2, 0, 1, 3).reshape(1, local_rows, QH * HD).astype(jnp.bfloat16)


def solution(mesh):
    placed = (
        P("dp", "ctx", None),
        P(("dp", "ctx"), None),
        P(),
        P("dp", "ctx", None),
        P("dp", "ctx"),
    )
    return jax.shard_map(
        per_device, mesh=mesh, in_specs=placed, out_specs=P("dp", "ctx", None), check_vma=False
    )
```

profile of v0, /device:TPU:0, one launch (start us, length us, event | category | flops | bytes accessed | tf_op | source)
XLA Modules:
  0.0 171.8 jit_solution(13662498133776428902)
XLA Ops:
  7.3 83.1 %all-gather.3.cloned.1.call-done = bf16[8192,512]{1,0:T(8,128)(2,1)} async-done(((bf16[256,512]{1,0:T(8,128)(2,1)}), bf16[8192,512]{1,0:T(8,128)(2,1)}) %all-gather.3.cloned.1.call-update) | async-done | bytes 8388624 | tf_op jit(solution)/shard_map/all_gather | solution.py:18
  90.4 5.8 %convolution_convert_fusion = bf16[128,1024]{1,0:T(8,128)(2,1)} fusion(bf16[512,1024]{1,0:T(8,128)(2,1)} %param.9, bf16[8192,512]{1,0:T(8,128)(2,1)} %all-gather.3.cloned.1.call-done, bf16[1,128,8192]{2,1,0:T(8,128)(2,1)S(1)} %copy-done), kind=kOutput, calls=%fused_computation.31 | convolution fusion | flops 1208156160 | bytes 11796480 | tf_op jit(solution)/shard_map/dot_general | solution.py:61
  97.7 7.3 %all-reduce = s32[16]{0:T(128)S(1)} all-reduce(s32[16]{0:T(128)S(1)} %bitcast_dynamic-update-slice_fusion), channel_id=1, replica_groups=mesh['dp'=4,'ctx'=8] {'ctx'}, use_global_device_ids=true, to_apply=%add | all-reduce | flops 16 | bytes 128
  105.1 1.6 copy.18
  106.7 1.3 copy.20
  108.7 14.3 %all-gather.5.cloned.1.call-done = bf16[1024,1024]{1,0:T(8,128)(2,1)} async-done(((bf16[128,1024]{1,0:T(8,128)(2,1)}), bf16[1024,1024]{1,0:T(8,128)(2,1)}) %all-gather.5.cloned.1.call-update) | async-done | bytes 2097168 | tf_op jit(solution)/shard_map/all_gather | solution.py:62
  122.9 38.1 %while.15 = (s32[]{:T(128)}, f32[4,8,128]{2,1,0:T(8,128)S(1)}, f32[4,8,128]{2,1,0:T(8,128)S(1)}, f32[4,8,128,128]{3,2,1,0:T(8,128)}, s32[4,256]{1,0:T(4,128)S(1)...) while((s32[]{:T(128)}, f32[4,8,128]{2,1,0:T(8,128)S(1)}, ...), condition=%wide.region_4.5_spmd.clone, body=%wide.region_1.4_spmd.clone.sunk | while | flops 552129792 | bytes 38670536 | solution.py:76
  122.9 1.3 fusion.55
  125.7 2.2 %fusion.57 = (f32[4,8,128]{2,1,0:T(8,128)S(1)}, f32[4,256,8,128]{3,1,2,0:T(8,128)S(1)}) fusion(pred[128,256]{0,1:T(8,128)(4,1)S(1)} %broadcast_compare_fusion.2, bf16[256,4,128,1]{0,2,3,1:T(8,128)(2,1)S(1)} %bitcast.71, bf16[4,8,128,128]{3,2,1,0:T(8,128)(2,1)} %get-tuple-element.223), kind=kOutput, calls=%fused_computation.3.clone.1 | convolution fusion | flops 271577088 | bytes 5554176 | tf_op jit(solution)/shard_map/while/body/eval_jaxpr/kgsd,tkd->kgst/dot_general | solution.py:39
  129.0 2.1 %fusion.60 = f32[4,8,128,128]{3,2,1,0:T(8,128)S(1)} fusion(f32[4,8,128,128]{3,2,1,0:T(8,128)S(1)} %copy-done.1, bf16[256,4,128,1]{0,2,3,1:T(8,128)(2,1)S(1)} %bitcast.72, f32[4,256,8,128]{3,1,2,0:T(8,128)S(1)} %get-tuple-element.191, f32[4,8,128]{2,1,0:T(8,128)S(1)} %select_maximum_fusion.2, pred[128,256]{0,1:T(8,128)(4,1)S(1)} %broadcast_compare_fusion.2, ...), kind=kOutput, calls=%fused_computation.8.clone.1 | convolution fusion | flops 275251200 | bytes 8716289 | tf_op jit(solution)/shard_map/while/body/eval_jaxpr/kgst,tkd->kgsd/dot_general | solution.py:48
  131.2 1.3 copy-done.2
  132.5 1.3 fusion.55
  135.2 2.2 %fusion.57 = (f32[4,8,128]{2,1,0:T(8,128)S(1)}, f32[4,256,8,128]{3,1,2,0:T(8,128)S(1)}) fusion(pred[128,256]{0,1:T(8,128)(4,1)S(1)} %broadcast_compare_fusion.2, bf16[256,4,128,1]{0,2,3,1:T(8,128)(2,1)S(1)} %bitcast.71, bf16[4,8,128,128]{3,2,1,0:T(8,128)(2,1)} %get-tuple-element.223), kind=kOutput, calls=%fused_computation.3.clone.1 | convolution fusion | flops 271577088 | bytes 5554176 | tf_op jit(solution)/shard_map/while/body/eval_jaxpr/kgsd,tkd->kgst/dot_general | solution.py:39
  138.6 2.1 %fusion.60 = f32[4,8,128,128]{3,2,1,0:T(8,128)S(1)} fusion(f32[4,8,128,128]{3,2,1,0:T(8,128)S(1)} %copy-done.1, bf16[256,4,128,1]{0,2,3,1:T(8,128)(2,1)S(1)} %bitcast.72, f32[4,256,8,128]{3,1,2,0:T(8,128)S(1)} %get-tuple-element.191, f32[4,8,128]{2,1,0:T(8,128)S(1)} %select_maximum_fusion.2, pred[128,256]{0,1:T(8,128)(4,1)S(1)} %broadcast_compare_fusion.2, ...), kind=kOutput, calls=%fused_computation.8.clone.1 | convolution fusion | flops 275251200 | bytes 8716289 | tf_op jit(solution)/shard_map/while/body/eval_jaxpr/kgst,tkd->kgsd/dot_general | solution.py:48
  140.7 1.3 copy-done.2
  142.0 1.3 fusion.55
  144.8 2.2 %fusion.57 = (f32[4,8,128]{2,1,0:T(8,128)S(1)}, f32[4,256,8,128]{3,1,2,0:T(8,128)S(1)}) fusion(pred[128,256]{0,1:T(8,128)(4,1)S(1)} %broadcast_compare_fusion.2, bf16[256,4,128,1]{0,2,3,1:T(8,128)(2,1)S(1)} %bitcast.71, bf16[4,8,128,128]{3,2,1,0:T(8,128)(2,1)} %get-tuple-element.223), kind=kOutput, calls=%fused_computation.3.clone.1 | convolution fusion | flops 271577088 | bytes 5554176 | tf_op jit(solution)/shard_map/while/body/eval_jaxpr/kgsd,tkd->kgst/dot_general | solution.py:39
  148.1 2.1 %fusion.60 = f32[4,8,128,128]{3,2,1,0:T(8,128)S(1)} fusion(f32[4,8,128,128]{3,2,1,0:T(8,128)S(1)} %copy-done.1, bf16[256,4,128,1]{0,2,3,1:T(8,128)(2,1)S(1)} %bitcast.72, f32[4,256,8,128]{3,1,2,0:T(8,128)S(1)} %get-tuple-element.191, f32[4,8,128]{2,1,0:T(8,128)S(1)} %select_maximum_fusion.2, pred[128,256]{0,1:T(8,128)(4,1)S(1)} %broadcast_compare_fusion.2, ...), kind=kOutput, calls=%fused_computation.8.clone.1 | convolution fusion | flops 275251200 | bytes 8716289 | tf_op jit(solution)/shard_map/while/body/eval_jaxpr/kgst,tkd->kgsd/dot_general | solution.py:48
  150.2 1.3 copy-done.2
  151.5 1.3 fusion.55
  154.3 2.2 %fusion.57 = (f32[4,8,128]{2,1,0:T(8,128)S(1)}, f32[4,256,8,128]{3,1,2,0:T(8,128)S(1)}) fusion(pred[128,256]{0,1:T(8,128)(4,1)S(1)} %broadcast_compare_fusion.2, bf16[256,4,128,1]{0,2,3,1:T(8,128)(2,1)S(1)} %bitcast.71, bf16[4,8,128,128]{3,2,1,0:T(8,128)(2,1)} %get-tuple-element.223), kind=kOutput, calls=%fused_computation.3.clone.1 | convolution fusion | flops 271577088 | bytes 5554176 | tf_op jit(solution)/shard_map/while/body/eval_jaxpr/kgsd,tkd->kgst/dot_general | solution.py:39
  157.6 2.1 %fusion.60 = f32[4,8,128,128]{3,2,1,0:T(8,128)S(1)} fusion(f32[4,8,128,128]{3,2,1,0:T(8,128)S(1)} %copy-done.1, bf16[256,4,128,1]{0,2,3,1:T(8,128)(2,1)S(1)} %bitcast.72, f32[4,256,8,128]{3,1,2,0:T(8,128)S(1)} %get-tuple-element.191, f32[4,8,128]{2,1,0:T(8,128)S(1)} %select_maximum_fusion.2, pred[128,256]{0,1:T(8,128)(4,1)S(1)} %broadcast_compare_fusion.2, ...), kind=kOutput, calls=%fused_computation.8.clone.1 | convolution fusion | flops 275251200 | bytes 8716289 | tf_op jit(solution)/shard_map/while/body/eval_jaxpr/kgst,tkd->kgsd/dot_general | solution.py:48
  159.7 1.3 copy-done.2
  161.0 1.9 %fusion.28 = bf16[128,4,8,128]{3,0,2,1:T(8,128)(2,1)S(1)} fusion(f32[4,8,128,128]{3,2,1,0:T(8,128)} %get-tuple-element.48, f32[4,8,128]{2,1,0:T(8,128)S(1)} %get-tuple-element.49), kind=kLoop, calls=%fused_computation.33 | loop fusion | flops 1048576 | bytes 3162112 | tf_op jit(solution)/shard_map/convert_element_type | solution.py:79
  (72 shorter events, 14.3 us)
Async XLA Ops:
  6.5 83.9 %copy-start = (bf16[1,128,8192]{2,1,0:T(8,128)(2,1)S(1)}, bf16[1,128,8192]{2,1,0:T(8,128)(2,1)}, u32[]{:S(2)}) copy-start(bf16[1,128,8192]{2,1,0:T(8,128)(2,1)} %param.7) | copy-start | bytes 6291460
  6.5 83.9 %all-gather.3.cloned.1.call-start = ((), (), s32[]{:S(2)}) async-start(), calls=%async_computation | async-start | bytes 8650752 | tf_op jit(solution)/shard_map/all_gather | solution.py:18
  7.3 89.0 %copy-start.4 = (u32[32]{0:T(128)S(1)}, u32[32]{0:T(128)}, u32[]{:S(2)}) copy-start(u32[32]{0:T(128)} %constant.71) | copy-start | bytes 388
  7.3 90.3 %copy-start.3 = (s32[1,2]{1,0:T(1,128)S(1)}, s32[1,2]{1,0:T(1,128)}, u32[]{:S(2)}) copy-start(s32[1,2]{1,0:T(1,128)} %param.11) | copy-start | bytes 28
  7.3 115.6 %all-gather.5.cloned.1.call-start = ((), (), s32[]{:S(2)}) async-start(), calls=%async_computation.1 | async-start | bytes 2359296 | tf_op jit(solution)/shard_map/all_gather | solution.py:62
  125.7 3.3 %copy-start.1 = (f32[4,8,128,128]{3,2,1,0:T(8,128)S(1)}, f32[4,8,128,128]{3,2,1,0:T(8,128)}, u32[]{:S(2)}) copy-start(f32[4,8,128,128]{3,2,1,0:T(8,128)} %get-tuple-element.209) | copy-start | bytes 6291460 | tf_op jit(solution)/shard_map/while
  131.2 1.3 copy-start.2
  135.2 3.3 %copy-start.1 = (f32[4,8,128,128]{3,2,1,0:T(8,128)S(1)}, f32[4,8,128,128]{3,2,1,0:T(8,128)}, u32[]{:S(2)}) copy-start(f32[4,8,128,128]{3,2,1,0:T(8,128)} %get-tuple-element.209) | copy-start | bytes 6291460 | tf_op jit(solution)/shard_map/while
  140.7 1.3 copy-start.2
  144.7 3.3 %copy-start.1 = (f32[4,8,128,128]{3,2,1,0:T(8,128)S(1)}, f32[4,8,128,128]{3,2,1,0:T(8,128)}, u32[]{:S(2)}) copy-start(f32[4,8,128,128]{3,2,1,0:T(8,128)} %get-tuple-element.209) | copy-start | bytes 6291460 | tf_op jit(solution)/shard_map/while
  150.2 1.3 copy-start.2
  154.3 3.3 %copy-start.1 = (f32[4,8,128,128]{3,2,1,0:T(8,128)S(1)}, f32[4,8,128,128]{3,2,1,0:T(8,128)}, u32[]{:S(2)}) copy-start(f32[4,8,128,128]{3,2,1,0:T(8,128)} %get-tuple-element.209) | copy-start | bytes 6291460 | tf_op jit(solution)/shard_map/while
  159.7 1.3 copy-start.2
Sparse Core Ops, SparseCore 0:
  10.2 80.1 all-gather.2
  96.4 26.4 all-gather.4
where the time goes:
time: 172 us
  waiting for transfers between devices  98.1 us (57%)
  matrix products  23.1 us (13%)
  local copies, waits for them, and re-layouts  16.7 us (10%)
  between operations  14.1 us (8%)
  other arithmetic  12 us (7%)
  blocking collectives  7.34 us (4%)
    all_gather x1, waiting for transfers between devices, per_device(): lax.all_gather(w_down, ('dp', 'ctx'), axis=0, tiled=True)  83.1 us
    all_gather x1, waiting for transfers between devices, per_device(): piece = lax.all_gather(kv_local, 'ctx', axis=0, tiled=True)  14.3 us
    dot_general x4, matrix products, update(): jnp.einsum('kgsd,tkd->kgst', query_heads, key_block, preferred_element_ty...  8.83 us
    dot_general x4, matrix products, update(): jnp.einsum('kgst,tkd->kgsd', expo.astype(jnp.bfloat16), value_block, pref...  8.43 us
    unnamed x1, blocking collectives  7.34 us
    dot_general x1, matrix products, per_device(): jnp.dot(latent, w_up, preferred_element_type=jnp.float32)  5.84 us
    dynamic_slice x12, local copies, waits for them, and re-layouts, per_device(): result, unused = lax.scan(step_block, start_state, (blocks, key_positions))  5.19 us
    while x20, local copies, waits for them, and re-layouts  5.18 us
  transfers between devices with their start and end apart: 2, of which 2 were waited for; matrix products, arithmetic and copies ran while one was open for 3% of the time, Pallas kernels for 0%

commit v1 on v0

--- a/solution.py
+++ b/solution.py
@@ -7,6 +7,12 @@
 QH = 32
 KVH = 4
 HD = 128
+
+
+def in_order(blocks, dim):
+    shape = list(blocks.shape[1:])
+    shape[dim] *= blocks.shape[0]
+    return jnp.moveaxis(blocks, 0, dim).reshape(shape)
 
 
 def per_device(tokens, w_down, w_up, queries, block_order):
@@ -59,7 +65,19 @@
         jnp.zeros((KVH, group, local_rows, HD), jnp.float32),
     )
     kv_local = jnp.dot(latent, w_up, preferred_element_type=jnp.float32).astype(jnp.bfloat16)
-    piece = lax.all_gather(kv_local, "ctx", axis=0, tiled=True)
+    size = lax.axis_size("ctx")
+    pairs = [(i, (i + 1) % size) for i in range(size)]
+    back = [(b, a) for a, b in pairs]
+    lower, upper = ([], [])
+    for step in range(size - 1):
+        if step % 2 == 0:
+            lower.append(lax.ppermute(lower[-1] if lower else kv_local, "ctx", pairs))
+        else:
+            upper.append(lax.ppermute(upper[-1] if upper else kv_local, "ctx", back))
+    pieces = jnp.stack([*lower[::-1], kv_local, *upper])
+    shift = lax.axis_index("ctx") - len(lower)
+    pieces = pieces[(jnp.arange(size) - shift) % size]
+    piece = in_order(pieces, 0)
     count = piece.shape[0]
     width = math.gcd(count, 256)
     blocks = piece.reshape(count // width, width, piece.shape[1])

time: 172 us -> 197 us (1.15)
  local copies, waits for them, and re-layouts: 16.7 us -> 33.9 us
  starting transfers between devices: 0.04 us -> 6.59 us
    ppermute x0 -> x7, waiting for transfers between devices: none -> 14.9 us  [the longest x3 8.1 us: per_device(): upper.append(lax.ppermute(upper[-1] if upper else kv_local, 'ctx', back))]
    all_gather x1 -> x0, waiting for transfers between devices: 14.3 us -> none  [per_device(): piece = lax.all_gather(kv_local, 'ctx', axis=0, tiled=True)]
    unnamed x11 -> x22, local copies, waits for them, and re-layouts: 3.63 us -> 14.4 us
    ppermute x0 -> x7, starting transfers between devices: none -> 6.59 us  [the longest x3 6.02 us: per_device(): upper.append(lax.ppermute(upper[-1] if upper else kv_local, 'ctx', back))]
    gather x0 -> x1, local copies, waits for them, and re-layouts: none -> 3.59 us  [per_device(): pieces = pieces[(jnp.arange(size) - shift) % size]]
    while x20, local copies, waits for them, and re-layouts: 5.18 us -> 7.22 us
  transfers between devices with their start and end apart: 2 -> 8, of which waited for: 2 -> 6; matrix products, arithmetic and copies ran while one was open for 3% -> 8% of each run, Pallas kernels for 0% -> 0%
where the time goes in v1:
time: 197 us; the launch traced here: 196 us
  waiting for transfers between devices  98.7 us (50%)
  local copies, waits for them, and re-layouts  33.9 us (17%)
  matrix products  21.8 us (11%)
  between operations  14.2 us (7%)
  other arithmetic  11.9 us (6%)
  blocking collectives  8.22 us (4%)
  starting transfers between devices  6.59 us (3%)
    all_gather x1, waiting for transfers between devices, per_device(): lax.all_gather(w_down, ('dp', 'ctx'), axis=0, tiled=True)  83.1 us
    unnamed x22, local copies, waits for them, and re-layouts  14.4 us
    dot_general x4, matrix products, update(): jnp.einsum('kgst,tkd->kgsd', expo.astype(jnp.bfloat16), value_block, pref...  8.42 us
    dot_general x4, matrix products, update(): jnp.einsum('kgsd,tkd->kgst', query_heads, key_block, preferred_element_ty...  8.22 us
    unnamed x1, blocking collectives  8.22 us
    ppermute x3, waiting for transfers between devices, per_device(): upper.append(lax.ppermute(upper[-1] if upper else kv_local, 'ctx', back))  8.1 us
    while x20, local copies, waits for them, and re-layouts  7.22 us
    ppermute x4, waiting for transfers between devices, per_device(): lower.append(lax.ppermute(lower[-1] if lower else kv_local, 'ctx', pairs))  6.79 us
  transfers between devices with their start and end apart: 8, of which 6 were waited for; matrix products, arithmetic and copies ran while one was open for 8% of the time, Pallas kernels for 0%

profile of v1, /device:TPU:0, one launch (start us, length us, event | category | flops | bytes accessed | tf_op | source)
XLA Modules:
  0.0 195.7 jit_solution(17988777057026347140)
XLA Ops:
  7.3 83.1 %all-gather.2.cloned.1.call-done = bf16[8192,512]{1,0:T(8,128)(2,1)} async-done(((bf16[256,512]{1,0:T(8,128)(2,1)}), bf16[8192,512]{1,0:T(8,128)(2,1)}) %all-gather.2.cloned.1.call-update) | async-done | bytes 8388624 | tf_op jit(solution)/shard_map/all_gather | solution.py:24
  90.4 5.1 %convolution_convert_fusion = bf16[128,1024]{1,0:T(8,128)(2,1)S(1)} fusion(bf16[512,1024]{1,0:T(8,128)(2,1)} %param.9, bf16[8192,512]{1,0:T(8,128)(2,1)} %all-gather.2.cloned.1.call-done, bf16[1,128,8192]{2,1,0:T(8,128)(2,1)S(1)} %copy-done), kind=kOutput, calls=%fused_computation.32 | convolution fusion | flops 1208156160 | bytes 11796480 | tf_op jit(solution)/shard_map/dot_general | solution.py:67
  97.2 5.1 %collective-permute-done = bf16[128,1024]{1,0:T(8,128)(2,1)S(1)} collective-permute-done((bf16[128,1024]{1,0:T(8,128)(2,1)S(1)}, bf16[128,1024]{1,0:T(8,128)(2,1)S(1)}, u32[]{:S(2)}, u32[]{:S(2)}) %collective-permute-start) | collective-permute-done | bytes 262176 | tf_op jit(solution)/shard_map/ppermute | solution.py:74
  102.3 8.2 %all-reduce = s32[16]{0:T(128)S(1)} all-reduce(s32[16]{0:T(128)S(1)} %bitcast_dynamic-update-slice_fusion.8), channel_id=1, replica_groups=mesh['dp'=4,'ctx'=8] {'ctx'}, use_global_device_ids=true, to_apply=%add | all-reduce | flops 16 | bytes 128
  111.8 5.5 %collective-permute-done.4 = bf16[128,1024]{1,0:T(8,128)(2,1)} collective-permute-done((bf16[128,1024]{1,0:T(8,128)(2,1)S(1)}, bf16[128,1024]{1,0:T(8,128)(2,1)}, u32[]{:S(2)}, u32[]{:S(2)}) %collective-permute-start.4) | collective-permute-done | bytes 262176 | tf_op jit(solution)/shard_map/ppermute | solution.py:76
  117.3 2.9 %collective-permute-start.5 = (bf16[128,1024]{1,0:T(8,128)(2,1)}, bf16[128,1024]{1,0:T(8,128)(2,1)}, u32[]{:S(2)}, u32[]{:S(2)}) collective-permute-start(bf16[128,1024]{1,0:T(8,128)(2,1)} %collective-permute-done.4), channel_id=1, source_target_pairs={{1,0},{2,1},{3,2},{4,3},{5,4},{6,5},{7,6},{0,7},{9,8},{10,9},{11,1... | collective-permute-start | bytes 786440 | tf_op jit(solution)/shard_map/ppermute | solution.py:76
  124.1 2.6 %collective-permute-done.5 = bf16[128,1024]{1,0:T(8,128)(2,1)} collective-permute-done((bf16[128,1024]{1,0:T(8,128)(2,1)}, bf16[128,1024]{1,0:T(8,128)(2,1)}, u32[]{:S(2)}, u32[]{:S(2)}) %collective-permute-start.5) | collective-permute-done | bytes 262176 | tf_op jit(solution)/shard_map/ppermute | solution.py:76
  126.7 2.8 %collective-permute-start.6 = (bf16[128,1024]{1,0:T(8,128)(2,1)}, bf16[128,1024]{1,0:T(8,128)(2,1)S(1)}, u32[]{:S(2)}, u32[]{:S(2)}) collective-permute-start(bf16[128,1024]{1,0:T(8,128)(2,1)} %collective-permute-done.5), channel_id=1, source_target_pairs={{1,0},{2,1},{3,2},{4,3},{5,4},{6,5},{7,6},{0,7},{9,8},{10,9},{11,1... | collective-permute-start | bytes 786440 | tf_op jit(solution)/shard_map/ppermute | solution.py:76
  132.1 1.7 bitcast_dynamic-update-slice_fusion.6
  133.7 1.7 bitcast_dynamic-update-slice_fusion.5
  135.4 1.7 bitcast_dynamic-update-slice_fusion.4
  137.8 1.7 bitcast_dynamic-update-slice_fusion.2
  139.5 1.7 bitcast_dynamic-update-slice_fusion.1
  141.9 3.6 %gather_fusion = bf16[8,128,1024]{2,1,0:T(8,128)(2,1)} fusion(bf16[8,128,1024]{2,1,0:T(8,128)(2,1)} %bitcast_dynamic-update-slice_fusion, s32[1024]{0:T(1024)S(1)} %pad_clamp_fusion), kind=kCustom, calls=%fused_computation | custom fusion | bytes 4194336 | tf_op jit(solution)/shard_map/gather | solution.py:79
  145.5 39.4 %while.15 = (s32[]{:T(128)}, f32[4,8,128]{2,1,0:T(8,128)S(1)}, f32[4,8,128]{2,1,0:T(8,128)S(1)}, f32[4,8,128,128]{3,2,1,0:T(8,128)}, s32[4,256]{1,0:T(4,128)S(1)...) while((s32[]{:T(128)}, f32[4,8,128]{2,1,0:T(8,128)S(1)}, ...), condition=%wide.region_4.5_spmd.clone, body=%wide.region_1.4_spmd.clone.sunk | while | flops 552129792 | bytes 38670536 | solution.py:94
  148.2 2.1 %fusion.59 = (f32[4,8,128]{2,1,0:T(8,128)S(1)}, f32[4,256,8,128]{3,1,2,0:T(8,128)S(1)}) fusion(pred[128,256]{0,1:T(8,128)(4,1)S(1)} %broadcast_compare_fusion.2, bf16[256,4,128,1]{0,2,3,1:T(8,128)(2,1)S(1)} %bitcast.89, bf16[4,8,128,128]{3,2,1,0:T(8,128)(2,1)} %get-tuple-element.223), kind=kOutput, calls=%fused_computation.4.clone.1 | convolution fusion | flops 271577088 | bytes 5554176 | tf_op jit(solution)/shard_map/while/body/eval_jaxpr/kgsd,tkd->kgst/dot_general | solution.py:45
  151.9 2.1 %fusion.62 = f32[4,8,128,128]{3,2,1,0:T(8,128)S(1)} fusion(f32[4,8,128,128]{3,2,1,0:T(8,128)S(1)} %copy-done.1, bf16[256,4,128,1]{0,2,3,1:T(8,128)(2,1)S(1)} %bitcast.91, f32[4,256,8,128]{3,1,2,0:T(8,128)S(1)} %get-tuple-element.191, f32[4,8,128]{2,1,0:T(8,128)S(1)} %select_maximum_fusion.2, pred[128,256]{0,1:T(8,128)(4,1)S(1)} %broadcast_compare_fusion.2, ...), kind=kOutput, calls=%fused_computation.9.clone.1 | convolution fusion | flops 275251200 | bytes 8716289 | tf_op jit(solution)/shard_map/while/body/eval_jaxpr/kgst,tkd->kgsd/dot_general | solution.py:54
  158.1 2.1 %fusion.59 = (f32[4,8,128]{2,1,0:T(8,128)S(1)}, f32[4,256,8,128]{3,1,2,0:T(8,128)S(1)}) fusion(pred[128,256]{0,1:T(8,128)(4,1)S(1)} %broadcast_compare_fusion.2, bf16[256,4,128,1]{0,2,3,1:T(8,128)(2,1)S(1)} %bitcast.89, bf16[4,8,128,128]{3,2,1,0:T(8,128)(2,1)} %get-tuple-element.223), kind=kOutput, calls=%fused_computation.4.clone.1 | convolution fusion | flops 271577088 | bytes 5554176 | tf_op jit(solution)/shard_map/while/body/eval_jaxpr/kgsd,tkd->kgst/dot_general | solution.py:45
  161.8 2.1 %fusion.62 = f32[4,8,128,128]{3,2,1,0:T(8,128)S(1)} fusion(f32[4,8,128,128]{3,2,1,0:T(8,128)S(1)} %copy-done.1, bf16[256,4,128,1]{0,2,3,1:T(8,128)(2,1)S(1)} %bitcast.91, f32[4,256,8,128]{3,1,2,0:T(8,128)S(1)} %get-tuple-element.191, f32[4,8,128]{2,1,0:T(8,128)S(1)} %select_maximum_fusion.2, pred[128,256]{0,1:T(8,128)(4,1)S(1)} %broadcast_compare_fusion.2, ...), kind=kOutput, calls=%fused_computation.9.clone.1 | convolution fusion | flops 275251200 | bytes 8716289 | tf_op jit(solution)/shard_map/while/body/eval_jaxpr/kgst,tkd->kgsd/dot_general | solution.py:54
  167.9 2.1 %fusion.59 = (f32[4,8,128]{2,1,0:T(8,128)S(1)}, f32[4,256,8,128]{3,1,2,0:T(8,128)S(1)}) fusion(pred[128,256]{0,1:T(8,128)(4,1)S(1)} %broadcast_compare_fusion.2, bf16[256,4,128,1]{0,2,3,1:T(8,128)(2,1)S(1)} %bitcast.89, bf16[4,8,128,128]{3,2,1,0:T(8,128)(2,1)} %get-tuple-element.223), kind=kOutput, calls=%fused_computation.4.clone.1 | convolution fusion | flops 271577088 | bytes 5554176 | tf_op jit(solution)/shard_map/while/body/eval_jaxpr/kgsd,tkd->kgst/dot_general | solution.py:45
  171.6 2.1 %fusion.62 = f32[4,8,128,128]{3,2,1,0:T(8,128)S(1)} fusion(f32[4,8,128,128]{3,2,1,0:T(8,128)S(1)} %copy-done.1, bf16[256,4,128,1]{0,2,3,1:T(8,128)(2,1)S(1)} %bitcast.91, f32[4,256,8,128]{3,1,2,0:T(8,128)S(1)} %get-tuple-element.191, f32[4,8,128]{2,1,0:T(8,128)S(1)} %select_maximum_fusion.2, pred[128,256]{0,1:T(8,128)(4,1)S(1)} %broadcast_compare_fusion.2, ...), kind=kOutput, calls=%fused_computation.9.clone.1 | convolution fusion | flops 275251200 | bytes 8716289 | tf_op jit(solution)/shard_map/while/body/eval_jaxpr/kgst,tkd->kgsd/dot_general | solution.py:54
  177.8 2.1 %fusion.59 = (f32[4,8,128]{2,1,0:T(8,128)S(1)}, f32[4,256,8,128]{3,1,2,0:T(8,128)S(1)}) fusion(pred[128,256]{0,1:T(8,128)(4,1)S(1)} %broadcast_compare_fusion.2, bf16[256,4,128,1]{0,2,3,1:T(8,128)(2,1)S(1)} %bitcast.89, bf16[4,8,128,128]{3,2,1,0:T(8,128)(2,1)} %get-tuple-element.223), kind=kOutput, calls=%fused_computation.4.clone.1 | convolution fusion | flops 271577088 | bytes 5554176 | tf_op jit(solution)/shard_map/while/body/eval_jaxpr/kgsd,tkd->kgst/dot_general | solution.py:45
  181.5 2.1 %fusion.62 = f32[4,8,128,128]{3,2,1,0:T(8,128)S(1)} fusion(f32[4,8,128,128]{3,2,1,0:T(8,128)S(1)} %copy-done.1, bf16[256,4,128,1]{0,2,3,1:T(8,128)(2,1)S(1)} %bitcast.91, f32[4,256,8,128]{3,1,2,0:T(8,128)S(1)} %get-tuple-element.191, f32[4,8,128]{2,1,0:T(8,128)S(1)} %select_maximum_fusion.2, pred[128,256]{0,1:T(8,128)(4,1)S(1)} %broadcast_compare_fusion.2, ...), kind=kOutput, calls=%fused_computation.9.clone.1 | convolution fusion | flops 275251200 | bytes 8716289 | tf_op jit(solution)/shard_map/while/body/eval_jaxpr/kgst,tkd->kgsd/dot_general | solution.py:54
  184.9 1.9 fusion.28
  (98 shorter events, 35.2 us)
Async XLA Ops:
  6.5 83.9 %copy-start = (bf16[1,128,8192]{2,1,0:T(8,128)(2,1)S(1)}, bf16[1,128,8192]{2,1,0:T(8,128)(2,1)}, u32[]{:S(2)}) copy-start(bf16[1,128,8192]{2,1,0:T(8,128)(2,1)} %param.7) | copy-start | bytes 6291460
  6.5 83.9 %all-gather.2.cloned.1.call-start = ((), (), s32[]{:S(2)}) async-start(), calls=%async_computation | async-start | bytes 8650752 | tf_op jit(solution)/shard_map/all_gather | solution.py:24
  7.3 88.6 %copy-start.6 = (u32[32]{0:T(128)S(1)}, u32[32]{0:T(128)}, u32[]{:S(2)}) copy-start(u32[32]{0:T(128)} %constant.94) | copy-start | bytes 388
  7.3 89.8 %copy-start.5 = (s32[1,2]{1,0:T(1,128)S(1)}, s32[1,2]{1,0:T(1,128)}, u32[]{:S(2)}) copy-start(s32[1,2]{1,0:T(1,128)} %param.11) | copy-start | bytes 28
  95.5 6.7 %collective-permute-start = (bf16[128,1024]{1,0:T(8,128)(2,1)S(1)}, bf16[128,1024]{1,0:T(8,128)(2,1)S(1)}, u32[]{:S(2)}, u32[]{:S(2)}) collective-permute-start(bf16[128,1024]{1,0:T(8,128)(2,1)S(1)} %convolution_convert_fusion), channel_id=1, source_target_pairs={{0,1},{1,2},{2,3},{3,4},{4,5},{5,6},{6,7},{7,0},{8,9},{9,10},{10,1... | collective-permute-start | bytes 786440 | tf_op jit(solution)/shard_map/ppermute | solution.py:74
  102.3 18.9 %copy-start.3 = (bf16[128,1024]{1,0:T(8,128)(2,1)}, bf16[128,1024]{1,0:T(8,128)(2,1)S(1)}, u32[]{:S(2)}) copy-start(bf16[128,1024]{1,0:T(8,128)(2,1)S(1)} %collective-permute-done) | copy-start | bytes 786436
  102.3 9.3 %collective-permute-start.1 = (bf16[128,1024]{1,0:T(8,128)(2,1)S(1)}, bf16[128,1024]{1,0:T(8,128)(2,1)S(1)}, u32[]{:S(2)}, u32[]{:S(2)}) collective-permute-start(bf16[128,1024]{1,0:T(8,128)(2,1)S(1)} %collective-permute-done), channel_id=1, source_target_pairs={{0,1},{1,2},{2,3},{3,4},{4,5},{5,6},{6,7},{7,0},{8,9},{9,10},{10,1... | collective-permute-start | bytes 786440 | tf_op jit(solution)/shard_map/ppermute | solution.py:74
  111.3 6.1 %collective-permute-start.4 = (bf16[128,1024]{1,0:T(8,128)(2,1)S(1)}, bf16[128,1024]{1,0:T(8,128)(2,1)}, u32[]{:S(2)}, u32[]{:S(2)}) collective-permute-start(bf16[128,1024]{1,0:T(8,128)(2,1)S(1)} %convolution_convert_fusion), channel_id=1, source_target_pairs={{1,0},{2,1},{3,2},{4,3},{5,4},{6,5},{7,6},{0,7},{9,8},{10,9},{11,1... | collective-permute-start | bytes 786440 | tf_op jit(solution)/shard_map/ppermute | solution.py:76
  111.6 9.6 %copy-start.4 = (bf16[128,1024]{1,0:T(8,128)(2,1)}, bf16[128,1024]{1,0:T(8,128)(2,1)S(1)}, u32[]{:S(2)}) copy-start(bf16[128,1024]{1,0:T(8,128)(2,1)S(1)} %collective-permute-done.1) | copy-start | bytes 786436
  111.6 9.6 %collective-permute-start.2 = (bf16[128,1024]{1,0:T(8,128)(2,1)S(1)}, bf16[128,1024]{1,0:T(8,128)(2,1)}, u32[]{:S(2)}, u32[]{:S(2)}) collective-permute-start(bf16[128,1024]{1,0:T(8,128)(2,1)S(1)} %collective-permute-done.1), channel_id=1, source_target_pairs={{0,1},{1,2},{2,3},{3,4},{4,5},{5,6},{6,7},{7,0},{8,9},{9,10},{10,1... | collective-permute-start | bytes 786440 | tf_op jit(solution)/shard_map/ppermute | solution.py:74
  117.3 9.4 %collective-permute-start.5 = (bf16[128,1024]{1,0:T(8,128)(2,1)}, bf16[128,1024]{1,0:T(8,128)(2,1)}, u32[]{:S(2)}, u32[]{:S(2)}) collective-permute-start(bf16[128,1024]{1,0:T(8,128)(2,1)} %collective-permute-done.4), channel_id=1, source_target_pairs={{1,0},{2,1},{3,2},{4,3},{5,4},{6,5},{7,6},{0,7},{9,8},{10,9},{11,1... | collective-permute-start | bytes 786440 | tf_op jit(solution)/shard_map/ppermute | solution.py:76
  121.1 9.3 %collective-permute-start.3 = (bf16[128,1024]{1,0:T(8,128)(2,1)}, bf16[128,1024]{1,0:T(8,128)(2,1)}, u32[]{:S(2)}, u32[]{:S(2)}) collective-permute-start(bf16[128,1024]{1,0:T(8,128)(2,1)} %collective-permute-done.2), channel_id=1, source_target_pairs={{0,1},{1,2},{2,3},{3,4},{4,5},{5,6},{6,7},{7,0},{8,9},{9,10},{10,1... | collective-permute-start | bytes 786440 | tf_op jit(solution)/shard_map/ppermute | solution.py:74
  126.7 14.4 %collective-permute-start.6 = (bf16[128,1024]{1,0:T(8,128)(2,1)}, bf16[128,1024]{1,0:T(8,128)(2,1)S(1)}, u32[]{:S(2)}, u32[]{:S(2)}) collective-permute-start(bf16[128,1024]{1,0:T(8,128)(2,1)} %collective-permute-done.5), channel_id=1, source_target_pairs={{1,0},{2,1},{3,2},{4,3},{5,4},{6,5},{7,6},{0,7},{9,8},{10,9},{11,1... | collective-permute-start | bytes 786440 | tf_op jit(solution)/shard_map/ppermute | solution.py:76
  150.3 1.6 copy-start.1
  154.0 1.3 copy-start.2
  160.2 1.6 copy-start.1
  163.9 1.3 copy-start.2
  170.0 1.6 copy-start.1
  173.7 1.3 copy-start.2
  179.9 1.6 copy-start.1
  183.6 1.3 copy-start.2
Sparse Core Ops, SparseCore 0:
  10.2 80.1 all-gather.1
